TPU v7x, 32 devices: a whole 2x2x4 slice. The times are simulated.
32 devices in a mesh: tm: 2 (over x), seq: 16 (over z, y, core).
Axes of the slice: x: 2, y: 2, z: 4, core: 2. Of those that a mesh axis runs over, the one named last changes fastest.
Arguments:
- tokens: bfloat16 [512, 5120], P(('tm', 'seq')), may hold values from -6 to 6
- w_query: bfloat16 [5120, 4096], P('seq'), may hold values from -0.078125 to 0.078125
- w_out: bfloat16 [4096, 5120], P(None, 'seq'), may hold values from -0.25 to 0.25
- k_cache: bfloat16 [4096, 4096], P(('tm', 'seq')), may hold values from -800 to 800
- v_cache: bfloat16 [4096, 4096], P(('tm', 'seq')), may hold values from -6 to 6
- radial_mask: int32 [16, 2, 32], replicated, may hold values from 0 to 1, as said below
- slot_frame: int32 [16], replicated, may hold values from 0 to 15, each once
Outputs:
- mixed: bfloat16 [512, 5120], P(('tm', 'seq'))
Inputs may be any that keep to these rules, and one draw needn't show every extreme that they name: radial_mask[f, b, f * 2 + b] = 1 for every frame f and tile b. `slot_frame`: each of the 16 frames is held by exactly one slot.
All inputs are finite; a program needn't handle non-finite values.
Results may differ from a plain program's by a relative error of at most 0.012.
The roundings to bfloat16 on the way count: a program that leaves them out, or rounds other values in their place, can miss the bound.
Values may be sent and summed in bfloat16 or wider, within the bound.
A program may use at most 128 MiB of HBM per device.

v0:
```python
import jax
import jax.numpy as jnp
from jax import lax
from jax.sharding import PartitionSpec as P

D = 5120
HD = 128
HEADS = 32
FRAMES = 16
BLOCK = 128
Q_DEV = 16


NEG = -1e30


def spread_columns(table, blocks, copies, groups):
    rows = table.shape[0]
    head_width = table.shape[1] // blocks
    grouped = table.reshape(rows, 1, blocks, 1, head_width)
    spread = jnp.broadcast_to(grouped, (rows, groups, blocks, copies, head_width))
    return spread.reshape(rows, groups * blocks * copies, head_width)


def on_device(tokens, w_query, w_out, k_cache, v_cache, radial_mask, slot_frame):
    seq_count = lax.axis_size("seq")
    group_count = lax.axis_size("tm")
    copies = max(1, seq_count // HEADS)
    per_dev = HEADS * copies // seq_count
    head_width = per_dev * HD
    blocks = seq_count // copies
    part_rows = Q_DEV // copies
    query_rows = part_rows * seq_count
    frame_tok = Q_DEV * seq_count
    frame_blocks = frame_tok // BLOCK
    per_group = FRAMES // group_count
    key_tile = 4 * BLOCK
    score_scale = HD ** (-0.5)
    my_seq = lax.axis_index("seq")
    my_group = lax.axis_index("tm")
    my_part = my_seq % copies
    split_rows = (
        tokens.reshape(copies, part_rows, D).transpose(1, 0, 2).reshape(part_rows, 1, copies, D)
    )
    token_send = jnp.broadcast_to(split_rows, (part_rows, blocks, copies, D)).reshape(
        part_rows, seq_count, D
    )
    query_send = spread_columns(w_query, blocks, copies, 1)
    frame = lax.dynamic_index_in_dim(slot_frame, my_group * per_group, 0, keepdims=False)
    onehot = (slot_frame[:, None] == lax.iota(jnp.int32, FRAMES)[None, :]).astype(jnp.float32)
    chosen = lax.dynamic_index_in_dim(radial_mask, frame, 0, keepdims=False).astype(jnp.float32)
    chosen = chosen.reshape(frame_blocks, FRAMES, frame_blocks)
    mask_slots = jnp.einsum("sf,qfb->qsb", onehot, chosen).reshape(
        frame_blocks, FRAMES * frame_blocks
    )
    row_index = lax.iota(jnp.int32, query_rows)
    token_index = row_index // part_rows * Q_DEV + my_part * part_rows + row_index % part_rows
    row_block = (token_index // BLOCK)[:, None] == lax.iota(jnp.int32, frame_blocks)[None, :]
    row_allowed = jnp.dot(
        row_block.astype(jnp.float32), mask_slots, preferred_element_type=jnp.float32
    )
    key_send = spread_columns(k_cache, blocks, copies, 1)
    value_send = spread_columns(v_cache, blocks, copies, 1)
    token_got, query_got, key_got, value_got = (
        lax.all_to_all(token_send, "seq", split_axis=1, concat_axis=0, tiled=True),
        lax.all_to_all(query_send, "seq", split_axis=1, concat_axis=0, tiled=True),
        lax.all_to_all(key_send, "seq", split_axis=1, concat_axis=0, tiled=True),
        lax.all_to_all(value_send, "seq", split_axis=1, concat_axis=0, tiled=True),
    )
    query = jnp.dot(
        token_got.reshape(query_rows, D),
        query_got.reshape(D, head_width),
        preferred_element_type=jnp.float32,
    )
    query = query.astype(jnp.bfloat16).reshape(query_rows, per_dev, HD)
    start_state = (
        jnp.full((query_rows, per_dev), NEG, jnp.float32),
        jnp.zeros((query_rows, per_dev), jnp.float32),
        jnp.zeros((query_rows, per_dev, HD), jnp.float32),
    )
    group_keys = key_got.reshape(-1, head_width)
    group_values = value_got.reshape(-1, head_width)
    keys = lax.all_gather(group_keys, "tm", axis=0, tiled=True)
    values = lax.all_gather(group_values, "tm", axis=0, tiled=True)
    tiles = keys.shape[0] // key_tile

    def one_tile(index, state):
        highest, denom, summed = state
        k_tile = lax.dynamic_slice_in_dim(keys, index * key_tile, key_tile, 0).reshape(
            key_tile, per_dev, HD
        )
        v_tile = lax.dynamic_slice_in_dim(values, index * key_tile, key_tile, 0).reshape(
            key_tile, per_dev, HD
        )
        first_block = index * key_tile // BLOCK
        allowed = lax.dynamic_slice_in_dim(row_allowed, first_block, key_tile // BLOCK, 1)
        keep = jnp.repeat(allowed > 0.5, BLOCK, axis=1)[:, None, :]
        scores = (
            jnp.einsum("qhd,khd->qhk", query, k_tile, preferred_element_type=jnp.float32)
            * score_scale
        )
        scores = jnp.where(keep, scores, NEG)
        new_high = jnp.maximum(highest, jnp.max(scores, axis=2))
        weights = jnp.where(keep, jnp.exp(scores - new_high[..., None]), 0.0)
        fade = jnp.exp(highest - new_high)
        denom = denom * fade + jnp.sum(weights, axis=2)
        update = jnp.einsum(
            "qhk,khd->qhd", weights.astype(jnp.bfloat16), v_tile, preferred_element_type=jnp.float32
        )
        summed = summed * fade[..., None] + update
        return (new_high, denom, summed)

    final_state = lax.fori_loop(0, tiles, one_tile, start_state)
    attended = (
        (final_state[2] / final_state[1][..., None])
        .astype(jnp.bfloat16)
        .reshape(query_rows, head_width)
    )
    out_columns = w_out.shape[1]
    every_head = lax.all_gather(attended[None], "seq", axis=0, tiled=True)
    every_head = every_head.reshape(blocks, copies, seq_count, part_rows, head_width)
    w_blocks = w_out.reshape(blocks, head_width, out_columns)
    columns = jnp.einsum(
        "bcsrw,bwo->scro", every_head, w_blocks, preferred_element_type=jnp.float32
    )
    columns = columns.reshape(frame_tok, out_columns).astype(jnp.bfloat16)
    mixed = lax.all_to_all(columns, "seq", split_axis=0, concat_axis=1, tiled=True)
    return mixed


def solution(mesh):
    return jax.shard_map(
        on_device,
        mesh=mesh,
        in_specs=(
            P(("tm", "seq"), None),
            P("seq", None),
            P(None, "seq"),
            P(("tm", "seq"), None),
            P(("tm", "seq"), None),
            P(),
            P(),
        ),
        out_specs=P(("tm", "seq"), None),
        check_vma=False,
    )
```

profile of v0, /device:TPU:0, one launch (start us, length us, event | category | flops | bytes accessed | tf_op | source)
XLA Modules:
  0.0 300.3 jit_solution(17684607203295914071)
XLA Ops:
  6.5 2.4 copy.52
  8.9 7.4 %all-to-all-start = ((bf16[128,16,256]{0,2,1:T(8,128)(2,1)}), bf16[128,16,256]{0,2,1:T(8,128)(2,1)S(1)}, u32[]{:S(2)}, u32[]{:S(2)}) async-start(bf16[128,16,256]{0,2,1:T(8,128)(2,1)} %bitcast.3), calls=%async_computation | async-start | bytes 2097152 | tf_op jit(solution)/shard_map/all_to_all | solution.py:67
  16.3 1.3 copy.55
  17.6 21.6 %all-to-all-done = bf16[128,16,256]{0,2,1:T(8,128)(2,1)S(1)} async-done(((bf16[128,16,256]{0,2,1:T(8,128)(2,1)}), bf16[128,16,256]{0,2,1:T(8,128)(2,1)S(1)}, u32[]{:S(2)}, u32[]{:S(2)}) %all-to-all-start) | async-done | bytes 1048608 | tf_op jit(solution)/shard_map/all_to_all | solution.py:67
  39.2 1.0 copy-done.1
  40.2 6.8 %all-to-all-start.3 = ((bf16[128,16,256]{0,2,1:T(8,128)(2,1)}), bf16[128,16,256]{0,2,1:T(8,128)(2,1)S(1)}, u32[]{:S(2)}, u32[]{:S(2)}) async-start(bf16[128,16,256]{0,2,1:T(8,128)(2,1)} %bitcast.14), calls=%async_computation.3 | async-start | bytes 2097152 | tf_op jit(solution)/shard_map/all_to_all | solution.py:68
  47.0 3.5 %copy.81 = bf16[40,16,8,256]{3,2,0,1:T(8,128)(2,1)} copy(bf16[40,16,8,256]{3,2,1,0:T(8,128)(2,1)} %bitcast.88) | data formatting | bytes 5242880 | tf_op jit(solution)/shard_map/reshape;reshape | solution.py:22
  50.5 19.4 %all-to-all-done.3 = bf16[128,16,256]{0,2,1:T(8,128)(2,1)S(1)} async-done(((bf16[128,16,256]{0,2,1:T(8,128)(2,1)}), bf16[128,16,256]{0,2,1:T(8,128)(2,1)S(1)}, u32[]{:S(2)}, u32[]{:S(2)}) %all-to-all-start.3) | async-done | bytes 1048608 | tf_op jit(solution)/shard_map/all_to_all | solution.py:68
  69.9 1.0 copy-done
  70.9 65.3 %all_to_all.76 = bf16[320,16,256]{2,0,1:T(8,128)(2,1)S(1)} all-to-all(bf16[320,16,256]{2,0,1:T(8,128)(2,1)} %bitcast.85), channel_id=1, replica_groups=mesh['tm'=2,'seq'=16] {'seq'}, dimensions={1} | all-to-all | bytes 5242880 | tf_op jit(solution)/shard_map/all_to_all | solution.py:66
  136.2 1.8 reshape.112
  138.1 5.2 %all-to-all-start.1 = ((bf16[16,16,5120]{2,0,1:T(8,128)(2,1)}), bf16[16,16,5120]{2,0,1:T(8,128)(2,1)}, u32[]{:S(2)}, u32[]{:S(2)}) async-start(bf16[16,16,5120]{2,0,1:T(8,128)(2,1)} %reshape.112), calls=%async_computation.1 | async-start | bytes 5242880 | tf_op jit(solution)/shard_map/all_to_all | solution.py:65
  143.4 2.3 copy.53
  145.7 2.3 copy.56
  151.9 41.6 %all-to-all-done.1 = bf16[16,16,5120]{2,0,1:T(8,128)(2,1)} async-done(((bf16[16,16,5120]{2,0,1:T(8,128)(2,1)}), bf16[16,16,5120]{2,0,1:T(8,128)(2,1)}, u32[]{:S(2)}, u32[]{:S(2)}) %all-to-all-start.1) | async-done | bytes 2621472 | tf_op jit(solution)/shard_map/all_to_all | solution.py:65
  193.5 2.9 convolution_convert_fusion
  196.5 18.4 %all-gather.6.cloned.1.call-done = bf16[4096,256]{1,0:T(8,128)(2,1)} async-done(((bf16[2048,256]{1,0:T(8,128)(2,1)}), bf16[4096,256]{1,0:T(8,128)(2,1)}) %all-gather.6.cloned.1.call-update) | async-done | bytes 2097168 | tf_op jit(solution)/shard_map/all_gather | solution.py:84
  214.9 20.1 %while.20 = (s32[]{:T(128)}, f32[256,2]{0,1:T(2,128)S(1)}, f32[256,2]{0,1:T(2,128)S(1)}, f32[256,2,128]{0,2,1:T(8,128)S(1)}, f32[256,32]{0,1:T(8,128)S(1)}, /*in...) while((s32[]{:T(128)}, f32[256,2]{0,1:T(2,128)S(1)}, ...), condition=%wide.region_3.4_spmd.clone, body=%wide.region_0.3_spmd.clone.sunk | while | flops 136777248 | bytes 6986118 | solution.py:113
  214.9 1.1 constant_dynamic-slice_fusion.3
  217.4 1.1 constant_dynamic-slice_fusion.3
  219.9 1.1 constant_dynamic-slice_fusion.3
  222.5 1.1 constant_dynamic-slice_fusion.3
  225.0 1.1 constant_dynamic-slice_fusion.3
  227.5 1.1 constant_dynamic-slice_fusion.3
  230.0 1.1 constant_dynamic-slice_fusion.3
  232.5 1.1 constant_dynamic-slice_fusion.3
  235.0 0.8 copy.67
  235.8 2.6 copy.73
  238.3 39.0 %all-gather.8.cloned.1.call-done = bf16[16,256,256]{2,1,0:T(8,128)(2,1)} async-done(((bf16[1,256,256]{2,1,0:T(8,128)(2,1)}), bf16[16,256,256]{2,1,0:T(8,128)(2,1)}) %all-gather.8.cloned.1.call-update) | async-done | bytes 2097168 | tf_op jit(solution)/shard_map/all_gather | solution.py:120
  277.4 3.3 %fusion.17 = bf16[16,16,320]{2,1,0:T(8,128)(2,1)S(1)} fusion(bf16[16,16,16,256]{3,2,1,0:T(8,128)(2,1)} %bitcast.94, bf16[16,256,320,1]{1,0,2,3:T(8,128)(2,1)S(1)} %bitcast.90), kind=kOutput, calls=%fused_computation.25 | convolution fusion | flops 671170560 | bytes 4882432 | tf_op jit(solution)/shard_map/bcsrw,bwo->scro/dot_general | solution.py:123
  280.7 12.2 %all_to_all.77 = bf16[16,16,320]{2,1,0:T(8,128)(2,1)S(1)} all-to-all(bf16[16,16,320]{2,1,0:T(8,128)(2,1)S(1)} %fusion.17), channel_id=1, replica_groups=mesh['tm'=2,'seq'=16] {'seq'}, dimensions={0} | all-to-all | bytes 327680 | tf_op jit(solution)/shard_map/all_to_all | solution.py:127
  292.9 0.8 all_to_all.70
  (109 shorter events, 13.0 us)
Async XLA Ops:
  6.5 9.8 %copy-start.2 = (bf16[128,4096]{1,0:T(8,128)(2,1)S(1)}, bf16[128,4096]{1,0:T(8,128)(2,1)}, u32[]{:S(2)}) copy-start(bf16[128,4096]{1,0:T(8,128)(2,1)} %param.13) | copy-start | bytes 3145732
  8.9 30.3 %all-to-all-start = ((bf16[128,16,256]{0,2,1:T(8,128)(2,1)}), bf16[128,16,256]{0,2,1:T(8,128)(2,1)S(1)}, u32[]{:S(2)}, u32[]{:S(2)}) async-start(bf16[128,16,256]{0,2,1:T(8,128)(2,1)} %bitcast.3), calls=%async_computation | async-start | bytes 2097152 | tf_op jit(solution)/shard_map/all_to_all | solution.py:67
  39.2 1.0 copy-start.1
  40.2 29.7 %all-to-all-start.3 = ((bf16[128,16,256]{0,2,1:T(8,128)(2,1)}), bf16[128,16,256]{0,2,1:T(8,128)(2,1)S(1)}, u32[]{:S(2)}, u32[]{:S(2)}) async-start(bf16[128,16,256]{0,2,1:T(8,128)(2,1)} %bitcast.14), calls=%async_computation.3 | async-start | bytes 2097152 | tf_op jit(solution)/shard_map/all_to_all | solution.py:68
  69.9 1.0 copy-start
  70.9 65.3 %copy-start.3 = (bf16[16,5120]{1,0:T(8,128)(2,1)S(1)}, bf16[16,5120]{1,0:T(8,128)(2,1)}, u32[]{:S(2)}) copy-start(bf16[16,5120]{1,0:T(8,128)(2,1)} %param.9) | copy-start | bytes 491524
  138.1 55.4 %all-to-all-start.1 = ((bf16[16,16,5120]{2,0,1:T(8,128)(2,1)}), bf16[16,16,5120]{2,0,1:T(8,128)(2,1)}, u32[]{:S(2)}, u32[]{:S(2)}) async-start(bf16[16,16,5120]{2,0,1:T(8,128)(2,1)} %reshape.112), calls=%async_computation.1 | async-start | bytes 5242880 | tf_op jit(solution)/shard_map/all_to_all | solution.py:65
  143.3 53.2 %all-gather.4.cloned.1.call-start = ((), (), s32[]{:S(2)}) async-start(), calls=%async_computation.5 | async-start | bytes 3145728 | tf_op jit(solution)/shard_map/all_gather | solution.py:83
  145.6 2.4 copy-start.4
  145.7 69.2 %all-gather.6.cloned.1.call-start = ((), (), s32[]{:S(2)}) async-start(), calls=%async_computation.6 | async-start | bytes 3145728 | tf_op jit(solution)/shard_map/all_gather | solution.py:84
  148.0 129.4 %all-gather.8.cloned.1.call-start = ((), (), s32[]{:S(2)}) async-start(), calls=%async_computation.7 | async-start | bytes 2228224 | tf_op jit(solution)/shard_map/all_gather | solution.py:120
Sparse Core Ops, SparseCore 0:
  145.8 34.3 all-gather.3
  181.7 33.0 all-gather.5
  235.9 41.4 all-gather.7
where the time goes:
time: 301 us; the launch traced here: 300 us
  waiting for transfers between devices  140 us (47%)
  blocking collectives  77.5 us (26%)
  local copies, waits for them, and re-layouts  32 us (11%)
  starting transfers between devices  19.5 us (6%)
  between operations  15 us (5%)
  matrix products  12.6 us (4%)
    all_to_all x1, blocking collectives, on_device(): lax.all_to_all(query_send, 'seq', split_axis=1, concat_axis=0, tiled=True)  65.3 us
    all_to_all x1, waiting for transfers between devices, on_device(): lax.all_to_all(token_send, 'seq', split_axis=1, concat_axis=0, tiled=True)  41.6 us
    all_gather x1, waiting for transfers between devices, on_device(): every_head = lax.all_gather(attended[None], 'seq', axis=0, tiled=True)  39 us
    all_to_all x1, waiting for transfers between devices, on_device(): lax.all_to_all(key_send, 'seq', split_axis=1, concat_axis=0, tiled=True)  21.6 us
    all_to_all x1, waiting for transfers between devices, on_device(): lax.all_to_all(value_send, 'seq', split_axis=1, concat_axis=0, tiled=True)  19.4 us
    all_gather x1, waiting for transfers between devices, on_device(): values = lax.all_gather(group_values, 'tm', axis=0, tiled=True)  18.4 us
    all_to_all x1, blocking collectives, on_device(): lax.all_to_all(columns, 'seq', split_axis=0, concat_axis=1, tiled=True)  12.2 us
    dynamic_slice x16, local copies, waits for them, and re-layouts, one_tile(): lax.dynamic_slice_in_dim(values, index * key_tile, key_tile, 0)  9.69 us
  transfers between devices with their start and end apart: 6, of which 5 were waited for; matrix products, arithmetic and copies ran while one was open for 6% of the time, Pallas kernels for 0%

commit v1 on v0

v1 whole, which is shorter than its diff:
```python
import functools

import jax
import jax.numpy as jnp
from jax import lax
from jax.experimental import pallas as pl
from jax.experimental.pallas import tpu as pltpu
from jax.sharding import PartitionSpec as P

HD = 128
HEADS = 32
FRAMES = 16
BLOCK = 128
KEY_SPLIT = 4
NEG = -1e30
FLOOR = -1e29
MESH = pl.DeviceIdType.MESH


def nt(a, b):
    return lax.dot_general(a, b, (((1,), (1,)), ((), ())), preferred_element_type=jnp.float32)


def tn(a, b):
    return lax.dot_general(a, b, (((0,), (0,)), ((), ())), preferred_element_type=jnp.float32)


def kernel(
    n_t, n_a, n_b,
    tok_ref, wq_ref, wo_ref, k_ref, v_ref, bias_ref,
    fin,
    tz, tg, wq, kg, vg, wo, qp, qr, qs, qa, s_buf, o_s, o_g, st_s, st_g, az_s, az, ag, cs,
    tz_s, tz_r, tg_s, tg_r, wq_s, wq_r, kg_s, kg_r, vg_s, vg_r, wo_r,
    qr_s, qr_r, qa_s, qa_r, os_s, os_r, ss_s, ss_r, az_ss, az_r, ag_s, ag_r, f_s, f_r,
):
    t = lax.axis_index("tm")
    s = lax.axis_index("seq")
    a = s // n_b
    b = lax.rem(s, n_b)
    n_p = n_t * n_b
    n_s = n_a * n_b
    h = t * n_b + b
    heads = qp.shape[0]
    width = heads * HD
    rows = tok_ref.shape[0]
    depth = tok_ref.shape[1] // n_a
    chunk = qp.shape[2]
    queries = n_a * chunk
    per_group = n_a // n_t
    sends = []

    def plane(d):
        g = lax.rem(h + d, n_p)
        return g, g // n_b, lax.rem(g, n_b)

    def cols(i, size):
        return pl.ds(pl.multiple_of(i * size, size), size)

    def send(src, dst, ss, rs, device):
        c = pltpu.make_async_remote_copy(
            src_ref=src, dst_ref=dst, send_sem=ss, recv_sem=rs,
            device_id=device, device_id_type=MESH,
        )
        c.start()
        sends.append(c)

    def landed(ref, sem):
        pltpu.make_async_copy(ref, ref, sem).wait()

    barrier = pltpu.get_barrier_semaphore()
    for d in range(1, n_p):
        g, t2, b2 = plane(d)
        pl.semaphore_signal(barrier, inc=1, device_id=(t2, a * n_b + b2), device_id_type=MESH)
    for da in range(1, n_a):
        for b2 in range(n_b):
            a2 = lax.rem(a + da, n_a)
            pl.semaphore_signal(barrier, inc=1, device_id=(t, a2 * n_b + b2), device_id_type=MESH)
    own = [
        pltpu.make_async_copy(tok_ref.at[:, cols(a, depth)], tz.at[a], tz_r.at[a]),
        pltpu.make_async_copy(wq_ref.at[:, cols(h, width)], wq.at[b], wq_r.at[b]),
        pltpu.make_async_copy(k_ref.at[:, cols(h, width)], kg.at[h], kg_r.at[h]),
        pltpu.make_async_copy(v_ref.at[:, cols(h, width)], vg.at[h], vg_r.at[h]),
    ]
    for c in own:
        c.start()
    wo_copy = pltpu.make_async_copy(wo_ref, wo, wo_r)
    wo_copy.start()
    pl.semaphore_wait(barrier, n_p - 1 + (n_a - 1) * n_b)

    for da in range(1, n_a):
        a2 = lax.rem(a + da, n_a)
        send(tok_ref.at[:, cols(a2, depth)], tz.at[a], tz_s.at[da], tz_r.at[a], (t, a2 * n_b + b))
    for db in range(1, n_b):
        b2 = lax.rem(b + db, n_b)
        send(
            wq_ref.at[:, cols(t * n_b + b2, width)], wq.at[b], wq_s.at[db], wq_r.at[b],
            (t, a * n_b + b2),
        )
    for i in range(n_a):
        landed(tz.at[i], tz_r.at[i])
    own_tok = pltpu.make_async_copy(tz, tg.at[t, :, b], tg_r.at[h])
    own_tok.start()
    for d in range(1, n_p):
        g, t2, b2 = plane(d)
        send(tz, tg.at[t, :, b], tg_s.at[d], tg_r.at[h], (t2, a * n_b + b2))
    for src, dst, ss, rs in ((k_ref, kg, kg_s, kg_r), (v_ref, vg, vg_s, vg_r)):
        for d in range(1, n_p):
            g, t2, b2 = plane(d)
            send(src.at[:, cols(g, width)], dst.at[h], ss.at[d], rs.at[h], (t2, a * n_b + b2))
    for i in range(n_b):
        landed(wq.at[i], wq_r.at[i])
    for i in range(n_p):
        landed(tg.at[i // n_b, :, i % n_b], tg_r.at[i])

    for j in range(heads):
        w_j = wq[:, :, j * HD:(j + 1) * HD].reshape(depth, HD)
        for c in range(n_a):
            piece = tg.at[c // per_group][
                (c % per_group) * (n_a // per_group):(c % per_group + 1) * (n_a // per_group)
            ]
            qp[j, c] = jnp.dot(
                piece.reshape(chunk, depth), w_j, preferred_element_type=jnp.float32
            )
        for da in range(1, n_a):
            a2 = lax.rem(a + da, n_a)
            send(
                qp.at[j, a2], qr.at[j, a], qr_s.at[j, da], qr_r.at[j, a], (t, a2 * n_b + b)
            )
        qr[j, a] = qp[j, a]
    for j in range(heads):
        for da in range(1, n_a):
            a2 = lax.rem(a + da, n_a)
            landed(qr.at[j, a2], qr_r.at[j, a2])
        total = qr[j, 0]
        for i in range(1, n_a):
            total = total + qr[j, i]
        total = total.astype(jnp.bfloat16)
        qs[j] = total
        for da in range(1, n_a):
            a2 = lax.rem(a + da, n_a)
            send(qs.at[j], qa.at[j, a], qa_s.at[j, da], qa_r.at[j, a], (t, a2 * n_b + b))
        qa[j, a] = total

    for i in range(n_p):
        landed(kg.at[i], kg_r.at[i])

    def attend(j):
        lanes = slice(j * HD, (j + 1) * HD)
        for da in range(1, n_a):
            a2 = lax.rem(a + da, n_a)
            landed(qa.at[j, a2], qa_r.at[j, a2])
        q_j = qa[j].reshape(queries, HD)

        def score(i, high):
            sc = nt(kg[i, :, lanes], q_j) * (HD ** -0.5) + bias_ref[pl.ds(i, 1), :]
            s_buf[i] = sc
            return jnp.maximum(high, jnp.max(sc, axis=0, keepdims=True))

        high = lax.fori_loop(0, n_p, score, jnp.full((1, queries), FLOOR, jnp.float32))
        if j == 0:
            for i in range(n_p):
                landed(vg.at[i], vg_r.at[i])

        def mix(i, state):
            denom, acc = state
            w = jnp.exp(s_buf[i] - high)
            return (
                denom + jnp.sum(w, axis=0, keepdims=True),
                acc + tn(vg[i, :, lanes], w.astype(jnp.bfloat16)),
            )

        denom, acc = lax.fori_loop(
            0, n_p, mix,
            (jnp.zeros((1, queries), jnp.float32), jnp.zeros((HD, queries), jnp.float32)),
        )
        out = (acc / jnp.where(denom > 0.0, denom, 1.0)).astype(jnp.bfloat16)
        for c in range(n_a):
            lo = c * chunk
            o_s[j, c] = out[:, lo:lo + chunk]
            st_s[j, c, 0:1] = high[:, lo:lo + chunk]
            st_s[j, c, 1:2] = denom[:, lo:lo + chunk]
            st_s[j, c, 2:8] = jnp.zeros((6, chunk), jnp.float32)
        for da in range(1, n_a):
            a2 = lax.rem(a + da, n_a)
            there = (t, a2 * n_b + b)
            send(o_s.at[j, a2], o_g.at[j, a], os_s.at[j, da], os_r.at[j, a], there)
            send(st_s.at[j, a2], st_g.at[j, a], ss_s.at[j, da], ss_r.at[j, a], there)
        o_g[j, a] = o_s[j, a]
        st_g[j, a] = st_s[j, a]

    def combine(j):
        for da in range(1, n_a):
            a2 = lax.rem(a + da, n_a)
            landed(o_g.at[j, a2], os_r.at[j, a2])
            landed(st_g.at[j, a2], ss_r.at[j, a2])
        high = st_g[j, 0, 0:1]
        for i in range(1, n_a):
            high = jnp.maximum(high, st_g[j, i, 0:1])
        den = jnp.zeros((1, chunk), jnp.float32)
        num = jnp.zeros((HD, chunk), jnp.float32)
        for i in range(n_a):
            w = st_g[j, i, 1:2] * jnp.exp(st_g[j, i, 0:1] - high)
            den = den + w
            num = num + w * o_g[j, i].astype(jnp.float32)
        res = jnp.transpose(num / den).astype(jnp.bfloat16)
        az_s[j] = res
        for da in range(1, n_a):
            a2 = lax.rem(a + da, n_a)
            send(az_s.at[j], az.at[j, a], az_ss.at[j, da], az_r.at[j, a], (t, a2 * n_b + b))
        az[j, a] = res

    def spread(j):
        for da in range(1, n_a):
            a2 = lax.rem(a + da, n_a)
            landed(az.at[j, a2], az_r.at[j, a2])
        for d in range(1, n_p):
            g, t2, b2 = plane(d)
            send(
                az.at[j, pl.ds(t2 * per_group, per_group)], ag.at[j, h],
                ag_s.at[j, d], ag_r.at[j, h], (t2, a * n_b + b2),
            )
        ag[j, h] = az[j, pl.ds(t * per_group, per_group)]

    for j in range(heads):
        attend(j)
        if j >= 1:
            combine(j - 1)
        if j >= 2:
            spread(j - 2)
    combine(heads - 1)
    if heads >= 2:
        spread(heads - 2)
    spread(heads - 1)

    wo_copy.wait()
    group_rows = per_group * chunk
    total = jnp.zeros((group_rows, wo.shape[1]), jnp.float32)
    for j in range(heads):
        for d in range(1, n_p):
            g, t2, b2 = plane(d)
            landed(ag.at[j, g], ag_r.at[j, g])

        def part(i, acc, j=j):
            at = pl.multiple_of(i * width + j * HD, HD)
            return acc + jnp.dot(
                ag[j, i].reshape(group_rows, HD), wo[pl.ds(at, HD), :],
                preferred_element_type=jnp.float32,
            )

        total = lax.fori_loop(0, n_p, part, total)
    cs[...] = total.astype(jnp.bfloat16).reshape(cs.shape)
    for d in range(1, n_s):
        s2 = lax.rem(s + d, n_s)
        send(cs.at[s2], fin.at[s], f_s.at[d], f_r.at[s], (t, s2))
    fin[s] = cs[s]
    for d in range(1, n_s):
        s2 = lax.rem(s + d, n_s)
        landed(fin.at[s2], f_r.at[s2])
    for c in sends:
        c.wait_send()


def on_device(tokens, w_query, w_out, k_cache, v_cache, radial_mask, slot_frame):
    n_s = lax.axis_size("seq")
    n_t = lax.axis_size("tm")
    n_a = KEY_SPLIT
    n_b = n_s // n_a
    n_p = n_t * n_b
    heads = HEADS // n_p
    width = heads * HD
    rows, d_model = tokens.shape
    depth = d_model // n_a
    queries = n_t * n_s * rows
    chunk = queries // n_a
    per_group = n_a // n_t
    keys = k_cache.shape[0]
    w_rows = w_query.shape[0]
    out_cols = w_out.shape[1]
    fb = radial_mask.shape[1]
    slots = slot_frame.shape[0]
    a = lax.axis_index("seq") // n_b

    onehot = (slot_frame[:, None] == lax.iota(jnp.int32, slots)[None, :]).astype(jnp.float32)
    frames = onehot.reshape(n_t, slots // n_t, slots)[:, 0]
    chosen = jnp.einsum("gf,fqk->gqk", frames, radial_mask.astype(jnp.float32))
    chosen = chosen.reshape(n_t * fb, slots, fb)
    by_slot = jnp.einsum("sf,qfb->sbq", onehot, chosen)
    tiles = by_slot.reshape(n_t, n_a, n_b, n_t * fb)
    mine = lax.dynamic_index_in_dim(tiles, a, 1, keepdims=False).reshape(n_p, n_t * fb)
    bias = jnp.repeat(jnp.where(mine > 0.5, 0.0, NEG), BLOCK, axis=1)

    bf, f32 = jnp.bfloat16, jnp.float32
    vm, dma = pltpu.VMEM, pltpu.SemaphoreType.DMA
    hbm = pl.BlockSpec(memory_space=pl.ANY)
    vmem = pl.BlockSpec(memory_space=pltpu.VMEM)
    got = pl.pallas_call(
        functools.partial(kernel, n_t, n_a, n_b),
        out_shape=jax.ShapeDtypeStruct((n_s, rows, out_cols), bf),
        in_specs=[hbm] * 5 + [vmem],
        out_specs=vmem,
        scratch_shapes=[
            vm((n_a, rows, depth), bf),
            vm((n_t, n_a, n_b, rows, depth), bf),
            vm((n_b, w_rows, width), bf),
            vm((n_p, keys, width), bf),
            vm((n_p, keys, width), bf),
            vm(w_out.shape, bf),
            vm((heads, n_a, chunk, HD), f32),
            vm((heads, n_a, chunk, HD), f32),
            vm((heads, chunk, HD), bf),
            vm((heads, n_a, chunk, HD), bf),
            vm((n_p, keys, queries), f32),
            vm((heads, n_a, HD, chunk), bf),
            vm((heads, n_a, HD, chunk), bf),
            vm((heads, n_a, 8, chunk), f32),
            vm((heads, n_a, 8, chunk), f32),
            vm((heads, chunk, HD), bf),
            vm((heads, n_a, chunk, HD), bf),
            vm((heads, n_p, per_group, chunk, HD), bf),
            vm((n_s, rows, out_cols), bf),
            dma((n_a,)), dma((n_a,)),
            dma((n_p,)), dma((n_p,)),
            dma((n_b,)), dma((n_b,)),
            dma((n_p,)), dma((n_p,)),
            dma((n_p,)), dma((n_p,)),
            dma,
            dma((heads, n_a)), dma((heads, n_a)),
            dma((heads, n_a)), dma((heads, n_a)),
            dma((heads, n_a)), dma((heads, n_a)),
            dma((heads, n_a)), dma((heads, n_a)),
            dma((heads, n_a)), dma((heads, n_a)),
            dma((heads, n_p)), dma((heads, n_p)),
            dma((n_s,)), dma((n_s,)),
        ],
        compiler_params=pltpu.CompilerParams(
            collective_id=0, has_side_effects=True, vmem_limit_bytes=60 * 1024 * 1024
        ),
    )(tokens, w_query, w_out, k_cache, v_cache, bias)
    return got.transpose(1, 0, 2).reshape(rows, n_s * out_cols)


def solution(mesh):
    return jax.shard_map(
        on_device,
        mesh=mesh,
        in_specs=(
            P(("tm", "seq"), None),
            P("seq", None),
            P(None, "seq"),
            P(("tm", "seq"), None),
            P(("tm", "seq"), None),
            P(),
            P(),
        ),
        out_specs=P(("tm", "seq"), None),
        check_vma=False,
    )
```

time: 301 us -> 138 us (0.46)
  waiting for transfers between devices: 140 us -> 0 us
  Pallas kernels: 0 us -> 128 us
  blocking collectives: 77.5 us -> 0 us
  local copies, waits for them, and re-layouts: 32 us -> 8.16 us
  starting transfers between devices: 19.5 us -> 0 us
  between operations: 15 us -> 0.03 us
  matrix products: 12.6 us -> 1.03 us
    pallas_call x0 -> x1, Pallas kernels: none -> 128 us  [on_device(): pl.pallas_call(functools.partial(kernel, n_t, n_a, n_b), out_shape=jax.Sh...]
    all_to_all x3 -> x0, waiting for transfers between devices: 82.6 us -> none  [the longest x1 41.6 us: on_device(): lax.all_to_all(token_send, 'seq', split_axis=1, concat_axis=0, tiled=True)]
    all_to_all x2 -> x0, blocking collectives: 77.5 us -> none  [the longest x1 65.3 us: on_device(): lax.all_to_all(query_send, 'seq', split_axis=1, concat_axis=0, tiled=True)]
    all_gather x3 -> x0, waiting for transfers between devices: 57.4 us -> none  [the longest x1 39 us: on_device(): every_head = lax.all_gather(attended[None], 'seq', axis=0, tiled=True)]
    all_to_all x3 -> x0, starting transfers between devices: 19.4 us -> none  [the longest x1 7.41 us: on_device(): lax.all_to_all(key_send, 'seq', split_axis=1, concat_axis=0, tiled=True)]
    dot_general x20 -> x2, matrix products: 12.6 us -> 1.03 us  [the longest x1 0.84 us: on_device(): by_slot = jnp.einsum('sf,qfb->sbq', onehot, chosen)]
    dynamic_slice x25 -> x0, local copies, waits for them, and re-layouts: 11.4 us -> none  [the longest x16 9.69 us: one_tile(): lax.dynamic_slice_in_dim(values, index * key_tile, key_tile, 0)]
    all_to_all x4 -> x0, local copies, waits for them, and re-layouts: 5.44 us -> none  [the longest x1 2.29 us: on_device(): lax.all_to_all(key_send, 'seq', split_axis=1, concat_axis=0, tiled=True)]
  transfers between devices with their start and end apart: 6 -> 0, of which waited for: 5 -> 0; matrix products, arithmetic and copies ran while one was open for 6% -> 0% of each run, Pallas kernels for 0% -> 0%
where the time goes in v1:
time: 138 us
  Pallas kernels  128 us (93%)
  local copies, waits for them, and re-layouts  8.16 us (6%)
    pallas_call x1, Pallas kernels, on_device(): pl.pallas_call(functools.partial(kernel, n_t, n_a, n_b), out_shape=jax.Sh...  128 us
    unnamed x2, local copies, waits for them, and re-layouts  4.64 us

profile of v1, /device:TPU:0, one launch (start us, length us, event | category | flops | bytes accessed | tf_op | source)
XLA Modules:
  0.0 137.6 jit_solution(1672168701378138753)
XLA Ops:
  0.0 0.7 eq.22
  0.7 0.1 copy.29
  0.8 0.7 convert_element_type.4
  1.6 0.2 fusion
  1.8 0.1 reshape.29
  1.9 0.8 fusion.3
  2.7 0.1 copy.19
  2.8 0.1 copy.25
  2.9 0.7 broadcast_bitcast_fusion.bias_ref
  3.6 4.5 %copy.21.wo_ref = bf16[4096,320]{1,0:T(8,128)(2,1)} copy(bf16[4096,320]{0,1:T(8,128)(2,1)} %param.9) | data formatting | bytes 5242880 | tf_op args[2]
  8.1 127.6 %shard_map.73 = bf16[16,16,320]{2,1,0:T(8,128)(2,1)} custom-call(bf16[16,5120]{1,0:T(8,128)(2,1)} %tok_ref.1, bf16[320,4096]{1,0:T(8,128)(2,1)} %wq_ref.1, bf16[4096,320]{1,0:T(8,128)(2,1)} %copy.21.wo_ref, bf16[128,4096]{1,0:T(8,128)(2,1)} %k_ref.1, bf16[128,4096]{1,0:T(8,128)(2,1)} %v_ref.1, f32[8,512]{1,0:T(8,128)} %broadcast_bitcast_fusion.bias_ref), custom_call_target="tpu_custom_call" | custom-call | tf_op jit(solution)/shard_map/pallas_call | solution.py:296
  135.8 1.0 copy.22
  136.7 0.8 reshape.32
  (3 shorter events, 0.0 us)

commit v2 on v1

--- a/solution.py
+++ b/solution.py
@@ -14,6 +14,7 @@
 KEY_SPLIT = 4
 NEG = -1e30
 FLOOR = -1e29
+CORES = 2
 MESH = pl.DeviceIdType.MESH
 
 
@@ -27,11 +28,11 @@
 
 def kernel(
     n_t, n_a, n_b,
-    tok_ref, wq_ref, wo_ref, k_ref, v_ref, bias_ref,
-    fin,
-    tz, tg, wq, kg, vg, wo, qp, qr, qs, qa, s_buf, o_s, o_g, st_s, st_g, az_s, az, ag, cs,
-    tz_s, tz_r, tg_s, tg_r, wq_s, wq_r, kg_s, kg_r, vg_s, vg_r, wo_r,
-    qr_s, qr_r, qa_s, qa_r, os_s, os_r, ss_s, ss_r, az_ss, az_r, ag_s, ag_r, f_s, f_r,
+    tok_ref, wq_ref, wo_ref, k_ref, v_ref, mask_ref, frame_ref,
+    out_ref,
+    bias_ref, fin, tz, tg, wq, kg, vg, wo, qp, qr, qs, qa, s_buf, o_s, o_g, st_s, st_g, az_s, az, ag, cs,
+    tz_s, tz_r, tg_s, tg_r, tf_s, wq_s, wq_r, kg_s, kg_r, vg_s, vg_r, wo_r,
+    qr_s, qr_r, qa_s, qa_r, os_s, os_r, ss_s, ss_r, az_ss, az_r, ag_s, ag_r, af_s, f_s, f_r,
 ):
     t = lax.axis_index("tm")
     s = lax.axis_index("seq")
@@ -53,6 +54,15 @@
         g = lax.rem(h + d, n_p)
         return g, g // n_b, lax.rem(g, n_b)
 
+    core = lax.rem(b, CORES)
+    mate = b - core + (CORES - 1 - core)
+    n_c = n_p // CORES
+    chip = h // CORES
+
+    def same_core(d):
+        g = lax.rem(chip + d, n_c) * CORES + core
+        return g, g // n_b, lax.rem(g, n_b)
+
     def cols(i, size):
         return pl.ds(pl.multiple_of(i * size, size), size)
 
@@ -100,17 +110,40 @@
         landed(tz.at[i], tz_r.at[i])
     own_tok = pltpu.make_async_copy(tz, tg.at[t, :, b], tg_r.at[h])
     own_tok.start()
-    for d in range(1, n_p):
-        g, t2, b2 = plane(d)
+    for d in range(1, n_c):
+        g, t2, b2 = same_core(d)
         send(tz, tg.at[t, :, b], tg_s.at[d], tg_r.at[h], (t2, a * n_b + b2))
+    send(tz, tg.at[t, :, b], tg_s.at[0], tg_r.at[h], (t, a * n_b + mate))
     for src, dst, ss, rs in ((k_ref, kg, kg_s, kg_r), (v_ref, vg, vg_s, vg_r)):
         for d in range(1, n_p):
             g, t2, b2 = plane(d)
             send(src.at[:, cols(g, width)], dst.at[h], ss.at[d], rs.at[h], (t2, a * n_b + b2))
+    slots = frame_ref.shape[0]
+    tiles = mask_ref.shape[1]
+
+    def allow(i, carry):
+        tile = (i // n_b) * n_s + a * n_b + lax.rem(i, n_b)
+        column = frame_ref[tile // tiles] * tiles + lax.rem(tile, tiles)
+        for g in range(n_t):
+            frame = frame_ref[g * (slots // n_t)]
+            for r in range(tiles):
+                lo = (g * tiles + r) * BLOCK
+                value = jnp.where(mask_ref[frame, r, column] > 0, 0.0, NEG)
+                bias_ref[i, :, lo:lo + BLOCK] = jnp.full((1, BLOCK), value, jnp.float32)
+        return carry
+
+    lax.fori_loop(0, n_p, allow, 0)
+    for d in range(1, n_c):
+        g, t2, b2 = same_core(d)
+        landed(tg.at[t2, :, b2], tg_r.at[g])
+        send(tg.at[t2, :, b2], tg.at[t2, :, b2], tf_s.at[d], tg_r.at[g], (t, a * n_b + mate))
     for i in range(n_b):
         landed(wq.at[i], wq_r.at[i])
-    for i in range(n_p):
-        landed(tg.at[i // n_b, :, i % n_b], tg_r.at[i])
+    landed(tg.at[t, :, b], tg_r.at[h])
+    for d in range(n_c):
+        g, t2, b2 = same_core(d)
+        b3 = b2 - core + (CORES - 1 - core)
+        landed(tg.at[t2, :, b3], tg_r.at[t2 * n_b + b3])
 
     for j in range(heads):
         w_j = wq[:, :, j * HD:(j + 1) * HD].reshape(depth, HD)
@@ -152,7 +185,7 @@
         q_j = qa[j].reshape(queries, HD)
 
         def score(i, high):
-            sc = nt(kg[i, :, lanes], q_j) * (HD ** -0.5) + bias_ref[pl.ds(i, 1), :]
+            sc = nt(kg[i, :, lanes], q_j) * (HD ** -0.5) + bias_ref[i]
             s_buf[i] = sc
             return jnp.maximum(high, jnp.max(sc, axis=0, keepdims=True))
 
@@ -213,13 +246,19 @@
         for da in range(1, n_a):
             a2 = lax.rem(a + da, n_a)
             landed(az.at[j, a2], az_r.at[j, a2])
-        for d in range(1, n_p):
-            g, t2, b2 = plane(d)
+        for d in range(n_c):
+            g, t2, b2 = same_core(d)
             send(
                 az.at[j, pl.ds(t2 * per_group, per_group)], ag.at[j, h],
-                ag_s.at[j, d], ag_r.at[j, h], (t2, a * n_b + b2),
+                ag_s.at[j, d], ag_r.at[j, h], (t2, a * n_b + (b2 if d else mate)),
             )
         ag[j, h] = az[j, pl.ds(t * per_group, per_group)]
+
+    def forward(j):
+        for d in range(1, n_c):
+            g, t2, b2 = same_core(d)
+            landed(ag.at[j, g], ag_r.at[j, g])
+            send(ag.at[j, g], ag.at[j, g], af_s.at[j, d], ag_r.at[j, g], (t, a * n_b + mate))
 
     for j in range(heads):
         attend(j)
@@ -227,25 +266,27 @@
             combine(j - 1)
         if j >= 2:
             spread(j - 2)
+        if j >= 3:
+            forward(j - 3)
     combine(heads - 1)
     if heads >= 2:
         spread(heads - 2)
     spread(heads - 1)
+    for j in range(max(0, heads - 3), heads):
+        forward(j)
 
     wo_copy.wait()
     group_rows = per_group * chunk
-    total = jnp.zeros((group_rows, wo.shape[1]), jnp.float32)
+    total = jnp.zeros((group_rows, wo.shape[0]), jnp.float32)
     for j in range(heads):
-        for d in range(1, n_p):
-            g, t2, b2 = plane(d)
-            landed(ag.at[j, g], ag_r.at[j, g])
+        for d in range(n_c):
+            g, t2, b2 = same_core(d)
+            g3 = g - core + (CORES - 1 - core)
+            landed(ag.at[j, g3], ag_r.at[j, g3])
 
         def part(i, acc, j=j):
             at = pl.multiple_of(i * width + j * HD, HD)
-            return acc + jnp.dot(
-                ag[j, i].reshape(group_rows, HD), wo[pl.ds(at, HD), :],
-                preferred_element_type=jnp.float32,
-            )
+            return acc + nt(ag[j, i].reshape(group_rows, HD), wo[:, pl.ds(at, HD)])
 
         total = lax.fori_loop(0, n_p, part, total)
     cs[...] = total.astype(jnp.bfloat16).reshape(cs.shape)
@@ -256,6 +297,9 @@
     for d in range(1, n_s):
         s2 = lax.rem(s + d, n_s)
         landed(fin.at[s2], f_r.at[s2])
+    wide = fin.shape[2]
+    for i in range(n_s):
+        out_ref[:, i * wide:(i + 1) * wide] = fin[i]
     for c in sends:
         c.wait_send()
 
@@ -276,35 +320,26 @@
     keys = k_cache.shape[0]
     w_rows = w_query.shape[0]
     out_cols = w_out.shape[1]
-    fb = radial_mask.shape[1]
-    slots = slot_frame.shape[0]
-    a = lax.axis_index("seq") // n_b
-
-    onehot = (slot_frame[:, None] == lax.iota(jnp.int32, slots)[None, :]).astype(jnp.float32)
-    frames = onehot.reshape(n_t, slots // n_t, slots)[:, 0]
-    chosen = jnp.einsum("gf,fqk->gqk", frames, radial_mask.astype(jnp.float32))
-    chosen = chosen.reshape(n_t * fb, slots, fb)
-    by_slot = jnp.einsum("sf,qfb->sbq", onehot, chosen)
-    tiles = by_slot.reshape(n_t, n_a, n_b, n_t * fb)
-    mine = lax.dynamic_index_in_dim(tiles, a, 1, keepdims=False).reshape(n_p, n_t * fb)
-    bias = jnp.repeat(jnp.where(mine > 0.5, 0.0, NEG), BLOCK, axis=1)
 
     bf, f32 = jnp.bfloat16, jnp.float32
     vm, dma = pltpu.VMEM, pltpu.SemaphoreType.DMA
     hbm = pl.BlockSpec(memory_space=pl.ANY)
     vmem = pl.BlockSpec(memory_space=pltpu.VMEM)
-    got = pl.pallas_call(
+    smem = pl.BlockSpec(memory_space=pltpu.SMEM)
+    return pl.pallas_call(
         functools.partial(kernel, n_t, n_a, n_b),
-        out_shape=jax.ShapeDtypeStruct((n_s, rows, out_cols), bf),
-        in_specs=[hbm] * 5 + [vmem],
+        out_shape=jax.ShapeDtypeStruct((rows, n_s * out_cols), bf),
+        in_specs=[hbm] * 5 + [smem] * 2,
         out_specs=vmem,
         scratch_shapes=[
+            vm((n_p, 1, queries), f32),
+            vm((n_s, rows, out_cols), bf),
             vm((n_a, rows, depth), bf),
             vm((n_t, n_a, n_b, rows, depth), bf),
             vm((n_b, w_rows, width), bf),
             vm((n_p, keys, width), bf),
             vm((n_p, keys, width), bf),
-            vm(w_out.shape, bf),
+            vm(w_out.shape[::-1], bf),
             vm((heads, n_a, chunk, HD), f32),
             vm((heads, n_a, chunk, HD), f32),
             vm((heads, chunk, HD), bf),
@@ -319,7 +354,7 @@
             vm((heads, n_p, per_group, chunk, HD), bf),
             vm((n_s, rows, out_cols), bf),
             dma((n_a,)), dma((n_a,)),
-            dma((n_p,)), dma((n_p,)),
+            dma((n_p,)), dma((n_p,)), dma((n_p,)),
             dma((n_b,)), dma((n_b,)),
             dma((n_p,)), dma((n_p,)),
             dma((n_p,)), dma((n_p,)),
@@ -329,14 +364,13 @@
             dma((heads, n_a)), dma((heads, n_a)),
             dma((heads, n_a)), dma((heads, n_a)),
             dma((heads, n_a)), dma((heads, n_a)),
-            dma((heads, n_p)), dma((heads, n_p)),
+            dma((heads, n_p)), dma((heads, n_p)), dma((heads, n_p)),
             dma((n_s,)), dma((n_s,)),
         ],
         compiler_params=pltpu.CompilerParams(
             collective_id=0, has_side_effects=True, vmem_limit_bytes=60 * 1024 * 1024
         ),
-    )(tokens, w_query, w_out, k_cache, v_cache, bias)
-    return got.transpose(1, 0, 2).reshape(rows, n_s * out_cols)
+    )(tokens, w_query, w_out.T, k_cache, v_cache, radial_mask, slot_frame)
 
 
 def solution(mesh):

time: 138 us -> 128 us (0.928)
  local copies, waits for them, and re-layouts: 8.16 us -> 1.59 us
  Pallas kernels: 128 us -> 126 us
    unnamed x2 -> x1, local copies, waits for them, and re-layouts: 4.64 us -> 1.59 us
    reshape x3 -> x0, local copies, waits for them, and re-layouts: 1.63 us -> none  [the longest x1 0.85 us: on_device(): return got.transpose(1, 0, 2).reshape(rows, n_s * out_cols)]
where the time goes in v2:
time: 128 us
  Pallas kernels  126 us (98%)
  local copies, waits for them, and re-layouts  1.59 us (1%)
    pallas_call x1, Pallas kernels, on_device(): pl.pallas_call(functools.partial(kernel, n_t, n_a, n_b), out_shape=jax.Sh...  126 us

profile of v2, /device:TPU:0, one launch (start us, length us, event | category | flops | bytes accessed | tf_op | source)
XLA Modules:
  0.0 127.9 jit_solution(16514077638515759602)
XLA Ops:
  0.0 126.3 %shard_map.73 = bf16[16,5120]{1,0:T(8,128)(2,1)} custom-call(bf16[16,5120]{1,0:T(8,128)(2,1)} %tok_ref.1, bf16[320,4096]{1,0:T(8,128)(2,1)} %wq_ref.1, bf16[320,4096]{1,0:T(8,128)(2,1)} %bitcast.1, bf16[128,4096]{1,0:T(8,128)(2,1)} %k_ref.1, bf16[128,4096]{1,0:T(8,128)(2,1)} %v_ref.1, s32[16,2,32]{2,1,0:T(2,128)} %mask_ref.1, s32[16]{0:T(128)} %frame_ref.1), custom_call_target="tpu_custom_call" | custom-call | tf_op jit(solution)/shard_map/pallas_call | solution.py:329
  126.3 1.6 %copy.9 = bf16[16,5120]{1,0:T(8,128)(2,1)} copy(bf16[16,5120]{1,0:T(8,128)(2,1)} %shard_map.73) | data formatting | bytes 327680

commit v3 on v2

--- a/solution.py
+++ b/solution.py
@@ -30,9 +30,9 @@
     n_t, n_a, n_b,
     tok_ref, wq_ref, wo_ref, k_ref, v_ref, mask_ref, frame_ref,
     out_ref,
-    bias_ref, fin, tz, tg, wq, kg, vg, wo, qp, qr, qs, qa, s_buf, o_s, o_g, st_s, st_g, az_s, az, ag, cs,
+    bias_ref, fin, tz, tg, wq, kg, vg, wo, qp, r1, x1, r2, qs, qa, s_buf, o_s, o_g, st_s, st_g, az_s, az, ag, cs,
     tz_s, tz_r, tg_s, tg_r, tf_s, wq_s, wq_r, kg_s, kg_r, vg_s, vg_r, wo_r,
-    qr_s, qr_r, qa_s, qa_r, os_s, os_r, ss_s, ss_r, az_ss, az_r, ag_s, ag_r, af_s, f_s, f_r,
+    r1_s, r1_r, r2_s, r2_r, qa_s, qa_r, os_s, os_r, ss_s, ss_r, az_ss, az_r, ag_s, ag_r, af_s, f_s, f_r,
 ):
     t = lax.axis_index("tm")
     s = lax.axis_index("seq")
@@ -45,9 +45,13 @@
     width = heads * HD
     rows = tok_ref.shape[0]
     depth = tok_ref.shape[1] // n_a
-    chunk = qp.shape[2]
+    chunk = qp.shape[3]
     queries = n_a * chunk
     per_group = n_a // n_t
+    low = lax.rem(a, 2)
+    high_half = a // 2
+    beside = (t, (2 * high_half + 1 - low) * n_b + b)
+    across = (t, (2 * (1 - high_half) + low) * n_b + b)
     sends = []
 
     def plane(d):
@@ -62,6 +66,9 @@
     def same_core(d):
         g = lax.rem(chip + d, n_c) * CORES + core
         return g, g // n_b, lax.rem(g, n_b)
+
+    def slab(j, g):
+        return ag.at[:, :, pl.ds(pl.multiple_of(g * width + j * HD, HD), HD)]
 
     def cols(i, size):
         return pl.ds(pl.multiple_of(i * size, size), size)
@@ -114,10 +121,6 @@
         g, t2, b2 = same_core(d)
         send(tz, tg.at[t, :, b], tg_s.at[d], tg_r.at[h], (t2, a * n_b + b2))
     send(tz, tg.at[t, :, b], tg_s.at[0], tg_r.at[h], (t, a * n_b + mate))
-    for src, dst, ss, rs in ((k_ref, kg, kg_s, kg_r), (v_ref, vg, vg_s, vg_r)):
-        for d in range(1, n_p):
-            g, t2, b2 = plane(d)
-            send(src.at[:, cols(g, width)], dst.at[h], ss.at[d], rs.at[h], (t2, a * n_b + b2))
     slots = frame_ref.shape[0]
     tiles = mask_ref.shape[1]
 
@@ -145,28 +148,28 @@
         b3 = b2 - core + (CORES - 1 - core)
         landed(tg.at[t2, :, b3], tg_r.at[t2 * n_b + b3])
 
+    for src, dst, ss, rs in ((k_ref, kg, kg_s, kg_r), (v_ref, vg, vg_s, vg_r)):
+        for d in range(1, n_p):
+            g, t2, b2 = plane(d)
+            send(src.at[:, cols(g, width)], dst.at[h], ss.at[d], rs.at[h], (t2, a * n_b + b2))
+
     for j in range(heads):
         w_j = wq[:, :, j * HD:(j + 1) * HD].reshape(depth, HD)
         for c in range(n_a):
             piece = tg.at[c // per_group][
                 (c % per_group) * (n_a // per_group):(c % per_group + 1) * (n_a // per_group)
             ]
-            qp[j, c] = jnp.dot(
+            qp[j, c // 2, c % 2] = jnp.dot(
                 piece.reshape(chunk, depth), w_j, preferred_element_type=jnp.float32
             )
-        for da in range(1, n_a):
-            a2 = lax.rem(a + da, n_a)
-            send(
-                qp.at[j, a2], qr.at[j, a], qr_s.at[j, da], qr_r.at[j, a], (t, a2 * n_b + b)
-            )
-        qr[j, a] = qp[j, a]
-    for j in range(heads):
-        for da in range(1, n_a):
-            a2 = lax.rem(a + da, n_a)
-            landed(qr.at[j, a2], qr_r.at[j, a2])
-        total = qr[j, 0]
-        for i in range(1, n_a):
-            total = total + qr[j, i]
+        send(qp.at[j, :, 1 - low], r1.at[j], r1_s.at[j], r1_r.at[j], beside)
+    for j in range(heads):
+        landed(r1.at[j], r1_r.at[j])
+        x1[j] = qp[j, 1 - high_half, low] + r1[j, 1 - high_half]
+        send(x1.at[j], r2.at[j], r2_s.at[j], r2_r.at[j], across)
+    for j in range(heads):
+        landed(r2.at[j], r2_r.at[j])
+        total = qp[j, high_half, low] + r1[j, high_half] + r2[j]
         total = total.astype(jnp.bfloat16)
         qs[j] = total
         for da in range(1, n_a):
@@ -249,16 +252,17 @@
         for d in range(n_c):
             g, t2, b2 = same_core(d)
             send(
-                az.at[j, pl.ds(t2 * per_group, per_group)], ag.at[j, h],
+                az.at[j, pl.ds(t2 * per_group, per_group)], slab(j, h),
                 ag_s.at[j, d], ag_r.at[j, h], (t2, a * n_b + (b2 if d else mate)),
             )
-        ag[j, h] = az[j, pl.ds(t * per_group, per_group)]
+        at = pl.multiple_of(h * width + j * HD, HD)
+        ag[:, :, pl.ds(at, HD)] = az[j, pl.ds(t * per_group, per_group)]
 
     def forward(j):
         for d in range(1, n_c):
             g, t2, b2 = same_core(d)
-            landed(ag.at[j, g], ag_r.at[j, g])
-            send(ag.at[j, g], ag.at[j, g], af_s.at[j, d], ag_r.at[j, g], (t, a * n_b + mate))
+            landed(slab(j, g), ag_r.at[j, g])
+            send(slab(j, g), slab(j, g), af_s.at[j, d], ag_r.at[j, g], (t, a * n_b + mate))
 
     for j in range(heads):
         attend(j)
@@ -277,18 +281,12 @@
 
     wo_copy.wait()
     group_rows = per_group * chunk
-    total = jnp.zeros((group_rows, wo.shape[0]), jnp.float32)
     for j in range(heads):
         for d in range(n_c):
             g, t2, b2 = same_core(d)
             g3 = g - core + (CORES - 1 - core)
-            landed(ag.at[j, g3], ag_r.at[j, g3])
-
-        def part(i, acc, j=j):
-            at = pl.multiple_of(i * width + j * HD, HD)
-            return acc + nt(ag[j, i].reshape(group_rows, HD), wo[:, pl.ds(at, HD)])
-
-        total = lax.fori_loop(0, n_p, part, total)
+            landed(slab(j, g3), ag_r.at[j, g3])
+    total = nt(ag[...].reshape(group_rows, n_p * width), wo[...])
     cs[...] = total.astype(jnp.bfloat16).reshape(cs.shape)
     for d in range(1, n_s):
         s2 = lax.rem(s + d, n_s)
@@ -340,8 +338,10 @@
             vm((n_p, keys, width), bf),
             vm((n_p, keys, width), bf),
             vm(w_out.shape[::-1], bf),
-            vm((heads, n_a, chunk, HD), f32),
-            vm((heads, n_a, chunk, HD), f32),
+            vm((heads, 2, 2, chunk, HD), f32),
+            vm((heads, 2, chunk, HD), f32),
+            vm((heads, chunk, HD), f32),
+            vm((heads, chunk, HD), f32),
             vm((heads, chunk, HD), bf),
             vm((heads, n_a, chunk, HD), bf),
             vm((n_p, keys, queries), f32),
@@ -351,7 +351,7 @@
             vm((heads, n_a, 8, chunk), f32),
             vm((heads, chunk, HD), bf),
             vm((heads, n_a, chunk, HD), bf),
-            vm((heads, n_p, per_group, chunk, HD), bf),
+            vm((per_group, chunk, n_p * width), bf),
             vm((n_s, rows, out_cols), bf),
             dma((n_a,)), dma((n_a,)),
             dma((n_p,)), dma((n_p,)), dma((n_p,)),
@@ -359,7 +359,7 @@
             dma((n_p,)), dma((n_p,)),
             dma((n_p,)), dma((n_p,)),
             dma,
-            dma((heads, n_a)), dma((heads, n_a)),
+            dma((heads,)), dma((heads,)), dma((heads,)), dma((heads,)),
             dma((heads, n_a)), dma((heads, n_a)),
             dma((heads, n_a)), dma((heads, n_a)),
             dma((heads, n_a)), dma((heads, n_a)),

time: 128 us -> 108 us (0.84)
  Pallas kernels: 126 us -> 106 us
    pallas_call x1, Pallas kernels: 126 us -> 106 us  [on_device(): pl.pallas_call(functools.partial(kernel, n_t, n_a, n_b), out_shape=jax.Sh...]
where the time goes in v3:
time: 108 us
  Pallas kernels  106 us (98%)
  local copies, waits for them, and re-layouts  1.59 us (1%)
    pallas_call x1, Pallas kernels, on_device(): pl.pallas_call(functools.partial(kernel, n_t, n_a, n_b), out_shape=jax.Sh...  106 us

profile of v3, /device:TPU:0, one launch (start us, length us, event | category | flops | bytes accessed | tf_op | source)
XLA Modules:
  0.0 107.7 jit_solution(5226603939220223214)
XLA Ops:
  0.0 106.1 %shard_map.73 = bf16[16,5120]{1,0:T(8,128)(2,1)} custom-call(bf16[16,5120]{1,0:T(8,128)(2,1)} %tok_ref.1, bf16[320,4096]{1,0:T(8,128)(2,1)} %wq_ref.1, bf16[320,4096]{1,0:T(8,128)(2,1)} %bitcast.1, bf16[128,4096]{1,0:T(8,128)(2,1)} %k_ref.1, bf16[128,4096]{1,0:T(8,128)(2,1)} %v_ref.1, s32[16,2,32]{2,1,0:T(2,128)} %mask_ref.1, s32[16]{0:T(128)} %frame_ref.1), custom_call_target="tpu_custom_call" | custom-call | tf_op jit(solution)/shard_map/pallas_call | solution.py:327
  106.1 1.6 %copy.9 = bf16[16,5120]{1,0:T(8,128)(2,1)} copy(bf16[16,5120]{1,0:T(8,128)(2,1)} %shard_map.73) | data formatting | bytes 327680

commit v4 on v3

--- a/solution.py
+++ b/solution.py
@@ -67,8 +67,19 @@
         g = lax.rem(chip + d, n_c) * CORES + core
         return g, g // n_b, lax.rem(g, n_b)
 
+    def head_cols(j, g):
+        return pl.ds(pl.multiple_of(g * width + j * HD, HD), HD)
+
     def slab(j, g):
-        return ag.at[:, :, pl.ds(pl.multiple_of(g * width + j * HD, HD), HD)]
+        return ag.at[:, :, head_cols(j, g)]
+
+    def send_weights(j):
+        for db in range(1, n_b):
+            b2 = lax.rem(b + db, n_b)
+            send(
+                wq_ref.at[:, head_cols(j, t * n_b + b2)], wq.at[j, b],
+                wq_s.at[j, db], wq_r.at[j, b], (t, a * n_b + b2),
+            )
 
     def cols(i, size):
         return pl.ds(pl.multiple_of(i * size, size), size)
@@ -94,10 +105,13 @@
             pl.semaphore_signal(barrier, inc=1, device_id=(t, a2 * n_b + b2), device_id_type=MESH)
     own = [
         pltpu.make_async_copy(tok_ref.at[:, cols(a, depth)], tz.at[a], tz_r.at[a]),
-        pltpu.make_async_copy(wq_ref.at[:, cols(h, width)], wq.at[b], wq_r.at[b]),
         pltpu.make_async_copy(k_ref.at[:, cols(h, width)], kg.at[h], kg_r.at[h]),
         pltpu.make_async_copy(v_ref.at[:, cols(h, width)], vg.at[h], vg_r.at[h]),
     ]
+    for j in range(heads):
+        own.append(pltpu.make_async_copy(
+            wq_ref.at[:, head_cols(j, h)], wq.at[j, b], wq_r.at[j, b]
+        ))
     for c in own:
         c.start()
     wo_copy = pltpu.make_async_copy(wo_ref, wo, wo_r)
@@ -107,12 +121,7 @@
     for da in range(1, n_a):
         a2 = lax.rem(a + da, n_a)
         send(tok_ref.at[:, cols(a2, depth)], tz.at[a], tz_s.at[da], tz_r.at[a], (t, a2 * n_b + b))
-    for db in range(1, n_b):
-        b2 = lax.rem(b + db, n_b)
-        send(
-            wq_ref.at[:, cols(t * n_b + b2, width)], wq.at[b], wq_s.at[db], wq_r.at[b],
-            (t, a * n_b + b2),
-        )
+    send_weights(0)
     for i in range(n_a):
         landed(tz.at[i], tz_r.at[i])
     own_tok = pltpu.make_async_copy(tz, tg.at[t, :, b], tg_r.at[h])
@@ -121,6 +130,8 @@
         g, t2, b2 = same_core(d)
         send(tz, tg.at[t, :, b], tg_s.at[d], tg_r.at[h], (t2, a * n_b + b2))
     send(tz, tg.at[t, :, b], tg_s.at[0], tg_r.at[h], (t, a * n_b + mate))
+    for j in range(1, heads):
+        send_weights(j)
     slots = frame_ref.shape[0]
     tiles = mask_ref.shape[1]
 
@@ -140,21 +151,21 @@
         g, t2, b2 = same_core(d)
         landed(tg.at[t2, :, b2], tg_r.at[g])
         send(tg.at[t2, :, b2], tg.at[t2, :, b2], tf_s.at[d], tg_r.at[g], (t, a * n_b + mate))
-    for i in range(n_b):
-        landed(wq.at[i], wq_r.at[i])
     landed(tg.at[t, :, b], tg_r.at[h])
     for d in range(n_c):
         g, t2, b2 = same_core(d)
         b3 = b2 - core + (CORES - 1 - core)
         landed(tg.at[t2, :, b3], tg_r.at[t2 * n_b + b3])
 
-    for src, dst, ss, rs in ((k_ref, kg, kg_s, kg_r), (v_ref, vg, vg_s, vg_r)):
-        for d in range(1, n_p):
-            g, t2, b2 = plane(d)
-            send(src.at[:, cols(g, width)], dst.at[h], ss.at[d], rs.at[h], (t2, a * n_b + b2))
-
     for j in range(heads):
-        w_j = wq[:, :, j * HD:(j + 1) * HD].reshape(depth, HD)
+        for i in range(n_b):
+            landed(wq.at[j, i], wq_r.at[j, i])
+        if j == heads - 1:
+            for src, dst, ss, rs in ((k_ref, kg, kg_s, kg_r), (v_ref, vg, vg_s, vg_r)):
+                for d in range(1, n_p):
+                    g, t2, b2 = plane(d)
+                    send(src.at[:, cols(g, width)], dst.at[h], ss.at[d], rs.at[h], (t2, a * n_b + b2))
+        w_j = wq[j].reshape(depth, HD)
         for c in range(n_a):
             piece = tg.at[c // per_group][
                 (c % per_group) * (n_a // per_group):(c % per_group + 1) * (n_a // per_group)
@@ -192,7 +203,9 @@
             s_buf[i] = sc
             return jnp.maximum(high, jnp.max(sc, axis=0, keepdims=True))
 
-        high = lax.fori_loop(0, n_p, score, jnp.full((1, queries), FLOOR, jnp.float32))
+        high = lax.fori_loop(
+            0, n_p, score, jnp.full((1, queries), FLOOR, jnp.float32), unroll=2
+        )
         if j == 0:
             for i in range(n_p):
                 landed(vg.at[i], vg_r.at[i])
@@ -208,6 +221,7 @@
         denom, acc = lax.fori_loop(
             0, n_p, mix,
             (jnp.zeros((1, queries), jnp.float32), jnp.zeros((HD, queries), jnp.float32)),
+            unroll=2,
         )
         out = (acc / jnp.where(denom > 0.0, denom, 1.0)).astype(jnp.bfloat16)
         for c in range(n_a):
@@ -240,15 +254,19 @@
             num = num + w * o_g[j, i].astype(jnp.float32)
         res = jnp.transpose(num / den).astype(jnp.bfloat16)
         az_s[j] = res
-        for da in range(1, n_a):
-            a2 = lax.rem(a + da, n_a)
-            send(az_s.at[j], az.at[j, a], az_ss.at[j, da], az_r.at[j, a], (t, a2 * n_b + b))
+        send(az_s.at[j], az.at[j, a], az_ss.at[j, 0], az_r.at[j, a], across)
+        send(az_s.at[j], az.at[j, a], az_ss.at[j, 1], az_r.at[j, a], beside)
         az[j, a] = res
 
+    def relay(j):
+        far = 2 * (1 - high_half) + low
+        landed(az.at[j, far], az_r.at[j, far])
+        send(az.at[j, far], az.at[j, far], az_ss.at[j, 2], az_r.at[j, far], beside)
+
     def spread(j):
-        for da in range(1, n_a):
-            a2 = lax.rem(a + da, n_a)
-            landed(az.at[j, a2], az_r.at[j, a2])
+        for half in range(2):
+            other = 2 * half + 1 - low
+            landed(az.at[j, other], az_r.at[j, other])
         for d in range(n_c):
             g, t2, b2 = same_core(d)
             send(
@@ -264,20 +282,12 @@
             landed(slab(j, g), ag_r.at[j, g])
             send(slab(j, g), slab(j, g), af_s.at[j, d], ag_r.at[j, g], (t, a * n_b + mate))
 
-    for j in range(heads):
-        attend(j)
-        if j >= 1:
-            combine(j - 1)
-        if j >= 2:
-            spread(j - 2)
-        if j >= 3:
-            forward(j - 3)
-    combine(heads - 1)
-    if heads >= 2:
-        spread(heads - 2)
-    spread(heads - 1)
-    for j in range(max(0, heads - 3), heads):
-        forward(j)
+    stages = (attend, combine, relay, spread, forward)
+    for step in range(heads + len(stages) - 1):
+        order = range(len(stages)) if step < heads else reversed(range(len(stages)))
+        for lag in order:
+            if 0 <= step - lag < heads:
+                stages[lag](step - lag)
 
     wo_copy.wait()
     group_rows = per_group * chunk
@@ -334,7 +344,7 @@
             vm((n_s, rows, out_cols), bf),
             vm((n_a, rows, depth), bf),
             vm((n_t, n_a, n_b, rows, depth), bf),
-            vm((n_b, w_rows, width), bf),
+            vm((heads, n_b, w_rows, HD), bf),
             vm((n_p, keys, width), bf),
             vm((n_p, keys, width), bf),
             vm(w_out.shape[::-1], bf),
@@ -355,7 +365,7 @@
             vm((n_s, rows, out_cols), bf),
             dma((n_a,)), dma((n_a,)),
             dma((n_p,)), dma((n_p,)), dma((n_p,)),
-            dma((n_b,)), dma((n_b,)),
+            dma((heads, n_b)), dma((heads, n_b)),
             dma((n_p,)), dma((n_p,)),
             dma((n_p,)), dma((n_p,)),
             dma,

time: 108 us -> 102 us (0.944)
  Pallas kernels: 106 us -> 100 us
    pallas_call x1, Pallas kernels: 106 us -> 100 us  [on_device(): pl.pallas_call(functools.partial(kernel, n_t, n_a, n_b), out_shape=jax.Sh...]
where the time goes in v4:
time: 102 us
  Pallas kernels  100 us (98%)
  local copies, waits for them, and re-layouts  1.59 us (2%)
    pallas_call x1, Pallas kernels, on_device(): pl.pallas_call(functools.partial(kernel, n_t, n_a, n_b), out_shape=jax.Sh...  100 us

profile of v4, /device:TPU:0, one launch (start us, length us, event | category | flops | bytes accessed | tf_op | source)
XLA Modules:
  0.0 102.1 jit_solution(1816704996616446971)
XLA Ops:
  0.0 100.5 %shard_map.73 = bf16[16,5120]{1,0:T(8,128)(2,1)} custom-call(bf16[16,5120]{1,0:T(8,128)(2,1)} %tok_ref.1, bf16[320,4096]{1,0:T(8,128)(2,1)} %wq_ref.1, bf16[320,4096]{1,0:T(8,128)(2,1)} %bitcast.1, bf16[128,4096]{1,0:T(8,128)(2,1)} %k_ref.1, bf16[128,4096]{1,0:T(8,128)(2,1)} %v_ref.1, s32[16,2,32]{2,1,0:T(2,128)} %mask_ref.1, s32[16]{0:T(128)} %frame_ref.1), custom_call_target="tpu_custom_call" | custom-call | tf_op jit(solution)/shard_map/pallas_call | solution.py:337
  100.5 1.6 %copy.9 = bf16[16,5120]{1,0:T(8,128)(2,1)} copy(bf16[16,5120]{1,0:T(8,128)(2,1)} %shard_map.73) | data formatting | bytes 327680

commit v5 on v4

--- a/solution.py
+++ b/solution.py
@@ -105,12 +105,16 @@
             pl.semaphore_signal(barrier, inc=1, device_id=(t, a2 * n_b + b2), device_id_type=MESH)
     own = [
         pltpu.make_async_copy(tok_ref.at[:, cols(a, depth)], tz.at[a], tz_r.at[a]),
-        pltpu.make_async_copy(k_ref.at[:, cols(h, width)], kg.at[h], kg_r.at[h]),
-        pltpu.make_async_copy(v_ref.at[:, cols(h, width)], vg.at[h], vg_r.at[h]),
     ]
     for j in range(heads):
         own.append(pltpu.make_async_copy(
             wq_ref.at[:, head_cols(j, h)], wq.at[j, b], wq_r.at[j, b]
+        ))
+        own.append(pltpu.make_async_copy(
+            k_ref.at[:, head_cols(j, h)], kg.at[j, h], kg_r.at[j, h]
+        ))
+        own.append(pltpu.make_async_copy(
+            v_ref.at[:, head_cols(j, h)], vg.at[j, h], vg_r.at[j, h]
         ))
     for c in own:
         c.start()
@@ -161,10 +165,14 @@
         for i in range(n_b):
             landed(wq.at[j, i], wq_r.at[j, i])
         if j == heads - 1:
-            for src, dst, ss, rs in ((k_ref, kg, kg_s, kg_r), (v_ref, vg, vg_s, vg_r)):
-                for d in range(1, n_p):
-                    g, t2, b2 = plane(d)
-                    send(src.at[:, cols(g, width)], dst.at[h], ss.at[d], rs.at[h], (t2, a * n_b + b2))
+            for i in range(heads):
+                for src, dst, ss, rs in ((k_ref, kg, kg_s, kg_r), (v_ref, vg, vg_s, vg_r)):
+                    for d in range(1, n_p):
+                        g, t2, b2 = plane(d)
+                        send(
+                            src.at[:, head_cols(i, g)], dst.at[i, h],
+                            ss.at[i, d], rs.at[i, h], (t2, a * n_b + b2),
+                        )
         w_j = wq[j].reshape(depth, HD)
         for c in range(n_a):
             piece = tg.at[c // per_group][
@@ -174,11 +182,13 @@
                 piece.reshape(chunk, depth), w_j, preferred_element_type=jnp.float32
             )
         send(qp.at[j, :, 1 - low], r1.at[j], r1_s.at[j], r1_r.at[j], beside)
-    for j in range(heads):
+
+    def reduce_pair(j):
         landed(r1.at[j], r1_r.at[j])
         x1[j] = qp[j, 1 - high_half, low] + r1[j, 1 - high_half]
         send(x1.at[j], r2.at[j], r2_s.at[j], r2_r.at[j], across)
-    for j in range(heads):
+
+    def reduce_across(j):
         landed(r2.at[j], r2_r.at[j])
         total = qp[j, high_half, low] + r1[j, high_half] + r2[j]
         total = total.astype(jnp.bfloat16)
@@ -188,34 +198,32 @@
             send(qs.at[j], qa.at[j, a], qa_s.at[j, da], qa_r.at[j, a], (t, a2 * n_b + b))
         qa[j, a] = total
 
-    for i in range(n_p):
-        landed(kg.at[i], kg_r.at[i])
-
     def attend(j):
-        lanes = slice(j * HD, (j + 1) * HD)
         for da in range(1, n_a):
             a2 = lax.rem(a + da, n_a)
             landed(qa.at[j, a2], qa_r.at[j, a2])
         q_j = qa[j].reshape(queries, HD)
 
+        for i in range(n_p):
+            landed(kg.at[j, i], kg_r.at[j, i])
+
         def score(i, high):
-            sc = nt(kg[i, :, lanes], q_j) * (HD ** -0.5) + bias_ref[i]
+            sc = nt(kg[j, i], q_j) * (HD ** -0.5) + bias_ref[i]
             s_buf[i] = sc
             return jnp.maximum(high, jnp.max(sc, axis=0, keepdims=True))
 
         high = lax.fori_loop(
             0, n_p, score, jnp.full((1, queries), FLOOR, jnp.float32), unroll=2
         )
-        if j == 0:
-            for i in range(n_p):
-                landed(vg.at[i], vg_r.at[i])
+        for i in range(n_p):
+            landed(vg.at[j, i], vg_r.at[j, i])
 
         def mix(i, state):
             denom, acc = state
             w = jnp.exp(s_buf[i] - high)
             return (
                 denom + jnp.sum(w, axis=0, keepdims=True),
-                acc + tn(vg[i, :, lanes], w.astype(jnp.bfloat16)),
+                acc + tn(vg[j, i], w.astype(jnp.bfloat16)),
             )
 
         denom, acc = lax.fori_loop(
@@ -282,9 +290,9 @@
             landed(slab(j, g), ag_r.at[j, g])
             send(slab(j, g), slab(j, g), af_s.at[j, d], ag_r.at[j, g], (t, a * n_b + mate))
 
-    stages = (attend, combine, relay, spread, forward)
+    stages = (reduce_pair, reduce_across, attend, combine, relay, spread, forward)
     for step in range(heads + len(stages) - 1):
-        order = range(len(stages)) if step < heads else reversed(range(len(stages)))
+        order = range(len(stages)) if step < heads + 2 else reversed(range(len(stages)))
         for lag in order:
             if 0 <= step - lag < heads:
                 stages[lag](step - lag)
@@ -345,8 +353,8 @@
             vm((n_a, rows, depth), bf),
             vm((n_t, n_a, n_b, rows, depth), bf),
             vm((heads, n_b, w_rows, HD), bf),
-            vm((n_p, keys, width), bf),
-            vm((n_p, keys, width), bf),
+            vm((heads, n_p, keys, HD), bf),
+            vm((heads, n_p, keys, HD), bf),
             vm(w_out.shape[::-1], bf),
             vm((heads, 2, 2, chunk, HD), f32),
             vm((heads, 2, chunk, HD), f32),
@@ -366,8 +374,8 @@
             dma((n_a,)), dma((n_a,)),
             dma((n_p,)), dma((n_p,)), dma((n_p,)),
             dma((heads, n_b)), dma((heads, n_b)),
-            dma((n_p,)), dma((n_p,)),
-            dma((n_p,)), dma((n_p,)),
+            dma((heads, n_p)), dma((heads, n_p)),
+            dma((heads, n_p)), dma((heads, n_p)),
             dma,
             dma((heads,)), dma((heads,)), dma((heads,)), dma((heads,)),
             dma((heads, n_a)), dma((heads, n_a)),

time: 102 us -> 104 us (1.020)
  Pallas kernels: 100 us -> 102 us
    pallas_call x1, Pallas kernels: 100 us -> 102 us  [on_device(): pl.pallas_call(functools.partial(kernel, n_t, n_a, n_b), out_shape=jax.Sh...]
where the time goes in v5:
time: 104 us
  Pallas kernels  102 us (98%)
  local copies, waits for them, and re-layouts  1.59 us (2%)
    pallas_call x1, Pallas kernels, on_device(): pl.pallas_call(functools.partial(kernel, n_t, n_a, n_b), out_shape=jax.Sh...  102 us

profile of v5, /device:TPU:0, one launch (start us, length us, event | category | flops | bytes accessed | tf_op | source)
XLA Modules:
  0.0 103.7 jit_solution(7481330253467559155)
XLA Ops:
  0.0 102.1 %shard_map.73 = bf16[16,5120]{1,0:T(8,128)(2,1)} custom-call(bf16[16,5120]{1,0:T(8,128)(2,1)} %tok_ref.1, bf16[320,4096]{1,0:T(8,128)(2,1)} %wq_ref.1, bf16[320,4096]{1,0:T(8,128)(2,1)} %bitcast.1, bf16[128,4096]{1,0:T(8,128)(2,1)} %k_ref.1, bf16[128,4096]{1,0:T(8,128)(2,1)} %v_ref.1, s32[16,2,32]{2,1,0:T(2,128)} %mask_ref.1, s32[16]{0:T(128)} %frame_ref.1), custom_call_target="tpu_custom_call" | custom-call | tf_op jit(solution)/shard_map/pallas_call | solution.py:345
  102.1 1.6 %copy.9 = bf16[16,5120]{1,0:T(8,128)(2,1)} copy(bf16[16,5120]{1,0:T(8,128)(2,1)} %shard_map.73) | data formatting | bytes 327680
